TPU v7x, 32 devices: a whole 2x2x4 slice. The times are simulated.
32 devices in a mesh: groups: 1, orient: 8 (over z, core), cls: 4 (over y, x).
Axes of the slice: x: 2, y: 2, z: 4, core: 2. Of those that a mesh axis runs over, the one named last changes fastest.
Arguments:
- particles: bfloat16 [384, 33024], P(('groups', 'orient', 'cls')), may hold values from -300 to 300
- projections: bfloat16 [8, 8, 33024], P('cls', 'orient')
- ctf: bfloat16 [8, 16512], replicated, may hold values from -1 to 1
- defocus_group: int32 [384], P(('groups', 'orient', 'cls')), may hold values from 0 to 7
- offsets: int32 [384, 2], P(('groups', 'orient', 'cls')), may hold values from -8 to 8
- routes: int32 [384, 4], P(('groups', 'orient', 'cls')), may hold values from 0 to 7, all different within a row; in each aligned block of 12 rows (0 to 11, 12 to 23, ...) at most 6 rows name the same one
Outputs:
- log_evidence: float32 [384], P(('groups', 'orient', 'cls'))
- data_sum: bfloat16 [8, 8, 33024], P(('groups', 'cls'), 'orient')
Inputs may be any that keep to these rules, and one draw needn't show every extreme that they name: `routes`: the 4 blocks of a particle differ; among the particles of one device no block is listed more than 6 times, and some block is listed exactly 6 times.
All inputs are finite; a program needn't handle non-finite values.
Results may differ from a plain program's by a relative error of at most 0.01.
The roundings to bfloat16 on the way count: a program that leaves them out, or rounds other values in their place, can miss the bound.
Values may be sent and summed in bfloat16 or wider, within the bound.
No kernel may reach another device: no remote copies, remote signals or barrier semaphores. Data moves between devices by JAX's collectives and lax.ppermute only.
A program may use at most 64 MiB of HBM per device.

v0:
```python
import math
import jax
import jax.numpy as jnp
import numpy as np
from jax import lax
from jax.sharding import PartitionSpec as P

KX = 86
KY = 192
BOX = 256
two_pi = 2.0 * math.pi
highest = lax.Precision.HIGHEST
local_across = np.array([0, 1, -1, 0, 0], dtype=np.int32)
local_down = np.array([0, 0, 0, 1, -1], dtype=np.int32)


def frequencies():
    column = jnp.arange(KX * KY, dtype=jnp.int32)
    return (column // KY, column % KY - KY // 2)


def rotation(shift_across, shift_down, freq_across, freq_down):
    turns = jnp.mod(freq_across * shift_across + freq_down * shift_down, BOX)
    angle = turns.astype(jnp.float32) * (two_pi / BOX)
    return (jnp.cos(angle), jnp.sin(angle))


def combine_stats(peaks, masses):
    top_value = jnp.max(peaks, axis=-1, keepdims=True)
    return top_value[..., 0] + jnp.log(jnp.sum(masses * jnp.exp(peaks - top_value), axis=-1))


def align_images(images, ctf_rows, shifts, freq_across, freq_down, pixel_count):
    real_part = images[:, :pixel_count].astype(jnp.float32)
    imag_part = images[:, pixel_count:].astype(jnp.float32)
    cos_base, sin_base = rotation(
        shifts[:, 0:1], shifts[:, 1:2], freq_across[None, :], freq_down[None, :]
    )
    first = (real_part * cos_base + imag_part * sin_base) * ctf_rows
    second = (imag_part * cos_base - real_part * sin_base) * ctf_rows
    return jnp.concatenate([first, second], axis=1).astype(jnp.bfloat16)


def spread_phase(table, ndim_rest):
    return table.reshape((table.shape[0],) + (1,) * ndim_rest + (table.shape[1],))


def turn_refs(ref_block, cos_shift, sin_shift, pixel_count):
    real_ref = ref_block[..., :pixel_count].astype(jnp.float32)
    imag_ref = ref_block[..., pixel_count:].astype(jnp.float32)
    cos_wide = spread_phase(cos_shift, real_ref.ndim - 1)
    sin_wide = spread_phase(sin_shift, real_ref.ndim - 1)
    first = real_ref[None] * cos_wide - imag_ref[None] * sin_wide
    second = real_ref[None] * sin_wide + imag_ref[None] * cos_wide
    turned = jnp.concatenate([first, second], axis=-1).astype(jnp.bfloat16)
    return (turned, real_ref * real_ref + imag_ref * imag_ref)


def back_rotate(summed, cos_shift, sin_shift, pixel_count):
    cos_wide = spread_phase(cos_shift, summed.ndim - 2)
    sin_wide = spread_phase(sin_shift, summed.ndim - 2)
    real_sum = summed[..., :pixel_count]
    imag_sum = summed[..., pixel_count:]
    first = jnp.sum(real_sum * cos_wide + imag_sum * sin_wide, axis=0)
    second = jnp.sum(imag_sum * cos_wide - real_sum * sin_wide, axis=0)
    return jnp.concatenate([first, second], axis=-1)


def slot_places(route_rows, orient_size):
    targets = route_rows.reshape(-1)
    onehot = (targets[:, None] == jnp.arange(orient_size, dtype=jnp.int32)[None, :]).astype(
        jnp.int32
    )
    before = jnp.cumsum(onehot, axis=0) - onehot
    return (targets, jnp.sum(before * onehot, axis=1))


def per_device(particles, projections, ctf, defocus_group, offsets, routes):
    pixel_count = KX * KY
    own_count = particles.shape[0]
    route_count = routes.shape[1]
    class_local = projections.shape[0]
    directions = projections.shape[1]
    group_count = ctf.shape[0]
    orient_size = lax.axis_size("orient")
    capacity = max(2, (own_count * route_count + orient_size - 1) // orient_size)
    total_slots = orient_size * capacity
    freq_across, freq_down = frequencies()
    ctf_table = ctf.astype(jnp.float32)
    group_onehot = (
        defocus_group[:, None] == jnp.arange(group_count, dtype=jnp.int32)[None, :]
    ).astype(jnp.float32)
    ctf_rows = jnp.dot(group_onehot, ctf_table, precision=highest)
    aligned = align_images(particles, ctf_rows, offsets, freq_across, freq_down, pixel_count)
    targets, orders = slot_places(routes, orient_size)
    slot_ids = targets * capacity + orders
    matches = (slot_ids[None, :] == jnp.arange(total_slots, dtype=jnp.int32)[:, None]).astype(
        jnp.int32
    )
    picked = jnp.sum(matches.reshape(total_slots, own_count, route_count), axis=2)
    send_images = jnp.dot(picked.astype(jnp.bfloat16), aligned, preferred_element_type=jnp.float32)
    send_images = send_images.astype(jnp.bfloat16).reshape(orient_size, capacity, 2 * pixel_count)
    send_codes = jnp.sum(picked * (defocus_group + 1)[None, :], axis=1).reshape(
        orient_size, capacity
    )
    tiles, codes = (
        lax.all_to_all(send_images, "orient", split_axis=0, concat_axis=0, tiled=True),
        lax.all_to_all(send_codes, "orient", split_axis=0, concat_axis=0, tiled=True),
    )
    rows_in = tiles.reshape(total_slots, 2 * pixel_count)
    codes_in = codes.reshape(total_slots)
    slot_groups = (
        codes_in[:, None] - 1 == jnp.arange(group_count, dtype=jnp.int32)[None, :]
    ).astype(jnp.float32)
    occupied = codes_in > 0
    cos_shift, sin_shift = rotation(
        jnp.asarray(local_across, dtype=jnp.int32)[:, None],
        jnp.asarray(local_down, dtype=jnp.int32)[:, None],
        freq_across[None, :],
        freq_down[None, :],
    )
    shift_total = cos_shift.shape[0]
    ctf_square = ctf_table * ctf_table
    ref_piece = lax.all_gather(projections, "cls", axis=0, tiled=True)
    piece_rows = ref_piece.shape[0]
    group_size = 2
    grouped = ref_piece.reshape(piece_rows // group_size, group_size, directions, 2 * pixel_count)

    def one_group(ref_block):
        turned, magnitude = turn_refs(ref_block, cos_shift, sin_shift, pixel_count)
        products = lax.dot_general(
            rows_in,
            turned.reshape(-1, 2 * pixel_count),
            (((1,), (1,)), ((), ())),
            preferred_element_type=jnp.float32,
        )
        energy = lax.dot_general(
            ctf_square,
            magnitude.reshape(group_size * directions, pixel_count),
            (((1,), (1,)), ((), ())),
            precision=highest,
        )
        slot_energy = jnp.dot(slot_groups, energy, precision=highest).reshape(
            total_slots, 1, group_size, directions
        )
        return (
            products.reshape(total_slots, shift_total, group_size, directions) - 0.5 * slot_energy
        )

    stacked = lax.map(one_group, grouped)
    scores = jnp.transpose(stacked, (1, 2, 0, 3, 4)).reshape(
        total_slots, shift_total, piece_rows, directions
    )
    slot_peak = jnp.max(scores, axis=(1, 2, 3))
    slot_mass = jnp.sum(jnp.exp(scores - slot_peak[:, None, None, None]), axis=(1, 2, 3))
    back_peak, back_mass = (
        lax.all_to_all(
            slot_peak.reshape(orient_size, capacity),
            "orient",
            split_axis=0,
            concat_axis=0,
            tiled=True,
        ),
        lax.all_to_all(
            slot_mass.reshape(orient_size, capacity),
            "orient",
            split_axis=0,
            concat_axis=0,
            tiled=True,
        ),
    )
    match_table = matches.astype(jnp.float32)
    entry_peak = jnp.dot(back_peak.reshape(-1), match_table, precision=highest).reshape(
        own_count, route_count
    )
    entry_mass = jnp.dot(back_mass.reshape(-1), match_table, precision=highest).reshape(
        own_count, route_count
    )
    log_evidence = combine_stats(entry_peak, entry_mass)
    slot_value = jnp.dot(picked.astype(jnp.float32), log_evidence, precision=highest).reshape(
        orient_size, capacity
    )
    evidence_in = lax.all_to_all(
        slot_value, "orient", split_axis=0, concat_axis=0, tiled=True
    ).reshape(total_slots)
    live = occupied[:, None, None, None]
    exponent = jnp.where(live, scores - evidence_in[:, None, None, None], 0.0)
    weights = jnp.where(live, jnp.exp(exponent), 0.0).astype(jnp.bfloat16)
    class_group_size = 2

    def one_group(group_index):
        weight_part = lax.dynamic_slice_in_dim(
            weights, group_index * class_group_size, class_group_size, 2
        )
        summed = lax.dot_general(
            weight_part.reshape(total_slots, -1),
            rows_in,
            (((0,), (0,)), ((), ())),
            preferred_element_type=jnp.float32,
        )
        summed = summed.reshape(shift_total, class_group_size, directions, 2 * pixel_count)
        return back_rotate(summed, cos_shift, sin_shift, pixel_count)

    results = lax.map(
        one_group,
        jnp.arange(class_local * lax.axis_size("cls") // class_group_size, dtype=jnp.int32),
    )
    data_sum = lax.psum_scatter(
        results.reshape(class_local * lax.axis_size("cls"), directions, 2 * pixel_count).astype(
            jnp.bfloat16
        ),
        "cls",
        scatter_dimension=0,
        tiled=True,
    )
    return (log_evidence, data_sum)


def solution(mesh):
    placed = (
        P(("groups", "orient", "cls"), None),
        P("cls", "orient", None),
        P(),
        P(("groups", "orient", "cls")),
        P(("groups", "orient", "cls"), None),
        P(("groups", "orient", "cls"), None),
    )
    return jax.shard_map(
        per_device,
        mesh=mesh,
        in_specs=placed,
        out_specs=(P(("groups", "orient", "cls")), P(("groups", "cls"), "orient", None)),
        check_vma=False,
    )
```

profile of v0, /device:TPU:0, one launch (start us, length us, event | category | flops | bytes accessed | tf_op | source)
XLA Modules:
  0.0 305.0 jit_solution(8616529737925251293)
XLA Ops:
  7.2 0.8 copy.40
  10.0 6.4 %all-to-all-start.1 = ((s32[8,1,6]{2,1,0:T(1,128)}), s32[8,1,6]{2,1,0:T(1,128)S(1)}, u32[]{:S(2)}, u32[]{:S(2)}) async-start(s32[8,1,6]{2,1,0:T(1,128)} %bitcast.3), calls=%async_computation.1 | async-start | bytes 8192 | tf_op jit(solution)/shard_map/all_to_all | solution.py:108
  17.8 6.1 %fusion.38 = (bf16[12,16512]{1,0:T(8,128)(2,1)S(1)}, bf16[12,16512]{1,0:T(8,128)(2,1)S(1)}) fusion(s32[12]{0:T(128)S(1)} %get-tuple-element.313, s32[16512]{0:T(1024)} %get-tuple-element.493, s32[12]{0:T(128)S(1)} %get-tuple-element.312, s32[16512]{0:T(1024)} %get-tuple-element.491, bf16[12,33024]{1,0:T(8,128)(2,1)} %param.12, bf16[8,16512]{1,0:T(8,128)(2,1)} %param.14, ...), kind=kOutput, calls=%fused_computation.63 | convolution fusion | flops 8718432 | bytes 1981584 | tf_op jit(solution)/shard_map/dot_general | solution.py:93
  23.9 1.0 convolution_convert_fusion
  24.9 2.6 reshape.281
  27.5 5.2 %all-to-all-start = ((bf16[8,6,33024]{2,1,0:T(8,128)(2,1)}), bf16[8,6,33024]{2,1,0:T(8,128)(2,1)}, u32[]{:S(2)}, u32[]{:S(2)}) async-start(bf16[8,6,33024]{2,1,0:T(8,128)(2,1)} %reshape.281), calls=%async_computation | async-start | bytes 8454144 | tf_op jit(solution)/shard_map/all_to_all | solution.py:107
  33.0 15.3 %all_gather.3 = bf16[8,1,33024]{2,1,0:T(2,128)(2,1)S(1)} all-gather(bf16[2,1,33024]{2,1,0:T(2,128)(2,1)S(1)} %copy.39), channel_id=1, replica_groups=mesh['groups'=1,'orient'=8,'cls'=4] {'cls'}, dimensions={0}, use_global_device_ids=true | all-gather | bytes 660480 | tf_op jit(solution)/shard_map/all_gather | solution.py:124
  48.2 3.2 %reduce.6 = bf16[8,33024]{1,0:T(8,128)(2,1)S(1)} reduce(bf16[8,1,33024]{2,1,0:T(2,128)(2,1)S(1)} %all_gather.3, bf16[]{:T(256)} %constant.106), dimensions={1}, to_apply=%all_gather.3.reduce_sub_computation | reduce | bytes 1056770 | tf_op jit(solution)/shard_map/all_gather | solution.py:124
  51.4 1.0 reshape.280
  52.4 0.9 convert_multiply_fusion.7
  53.4 74.1 %all-to-all-done = bf16[8,6,33024]{2,1,0:T(8,128)(2,1)} async-done(((bf16[8,6,33024]{2,1,0:T(8,128)(2,1)}), bf16[8,6,33024]{2,1,0:T(8,128)(2,1)}, u32[]{:S(2)}, u32[]{:S(2)}) %all-to-all-start) | async-done | bytes 3170336 | tf_op jit(solution)/shard_map/all_to_all | solution.py:107
  127.5 2.8 reshape.282
  130.4 57.9 %while.24 = (s32[]{:T(128)}, f32[4,48,5,2,1]{1,3,2,4,0:T(2,128)S(1)}, bf16[4,2,1,33024]{3,1,2,0:T(2,128)(2,1)}, bf16[48,33024]{1,0:T(8,128)(2,1)S(1)}, f32[8,165...) while((s32[]{:T(128)}, ...), condition=%wide.region_5.6_spmd.clone.clone, body=%wide.region_4.5_spmd.clone.clone.sunk | while | flops 39077952 | bytes 9925141 | solution.py:150
  130.4 3.1 %fusion.95 = (f32[5,16512]{1,0:T(8,128)S(1)}, f32[5,16512]{1,0:T(8,128)S(1)}) fusion(s32[5]{0:T(128)S(1)} %get-tuple-element.481, s32[16512]{0:T(1024)} %get-tuple-element.482, s32[5]{0:T(128)S(1)} %get-tuple-element.479, s32[16512]{0:T(1024)} %get-tuple-element.480), kind=kLoop, calls=%fused_computation.20.clone.1 | loop fusion | flops 1320960 | bytes 792616 | tf_op jit(solution)/shard_map/cos | solution.py:25
  133.5 1.0 dynamic-slice_bitcast_fusion.2
  135.1 1.4 subtract_convert_fusion.2
  136.5 2.3 add.652
  138.8 1.3 sub.142
  140.1 2.1 convolution_bitcast_fusion.5
  142.3 2.3 fusion.96
  144.9 3.1 %fusion.95 = (f32[5,16512]{1,0:T(8,128)S(1)}, f32[5,16512]{1,0:T(8,128)S(1)}) fusion(s32[5]{0:T(128)S(1)} %get-tuple-element.481, s32[16512]{0:T(1024)} %get-tuple-element.482, s32[5]{0:T(128)S(1)} %get-tuple-element.479, s32[16512]{0:T(1024)} %get-tuple-element.480), kind=kLoop, calls=%fused_computation.20.clone.1 | loop fusion | flops 1320960 | bytes 792616 | tf_op jit(solution)/shard_map/cos | solution.py:25
  148.0 1.0 dynamic-slice_bitcast_fusion.2
  149.6 1.4 subtract_convert_fusion.2
  151.0 2.3 add.652
  153.3 1.3 sub.142
  154.6 2.1 convolution_bitcast_fusion.5
  156.8 2.3 fusion.96
  159.4 3.1 %fusion.95 = (f32[5,16512]{1,0:T(8,128)S(1)}, f32[5,16512]{1,0:T(8,128)S(1)}) fusion(s32[5]{0:T(128)S(1)} %get-tuple-element.481, s32[16512]{0:T(1024)} %get-tuple-element.482, s32[5]{0:T(128)S(1)} %get-tuple-element.479, s32[16512]{0:T(1024)} %get-tuple-element.480), kind=kLoop, calls=%fused_computation.20.clone.1 | loop fusion | flops 1320960 | bytes 792616 | tf_op jit(solution)/shard_map/cos | solution.py:25
  162.4 1.0 dynamic-slice_bitcast_fusion.2
  164.1 1.4 subtract_convert_fusion.2
  165.5 2.3 add.652
  167.8 1.3 sub.142
  169.1 2.1 convolution_bitcast_fusion.5
  171.3 2.3 fusion.96
  173.8 3.1 %fusion.95 = (f32[5,16512]{1,0:T(8,128)S(1)}, f32[5,16512]{1,0:T(8,128)S(1)}) fusion(s32[5]{0:T(128)S(1)} %get-tuple-element.481, s32[16512]{0:T(1024)} %get-tuple-element.482, s32[5]{0:T(128)S(1)} %get-tuple-element.479, s32[16512]{0:T(1024)} %get-tuple-element.480), kind=kLoop, calls=%fused_computation.20.clone.1 | loop fusion | flops 1320960 | bytes 792616 | tf_op jit(solution)/shard_map/cos | solution.py:25
  176.9 1.0 dynamic-slice_bitcast_fusion.2
  178.6 1.4 subtract_convert_fusion.2
  180.0 2.3 add.652
  182.3 1.3 sub.142
  183.6 2.1 convolution_bitcast_fusion.5
  185.8 2.3 fusion.96
  189.1 3.3 %all-to-all-start.3 = ((f32[8,1,6]{2,1,0:T(1,128)}), f32[8,1,6]{2,1,0:T(1,128)S(1)}, u32[]{:S(2)}, u32[]{:S(2)}) async-start(f32[8,1,6]{2,1,0:T(1,128)} %bitcast.8), calls=%async_computation.3 | async-start | bytes 8192 | tf_op jit(solution)/shard_map/all_to_all | solution.py:164
  193.2 4.7 %all-to-all-done.3 = f32[8,1,6]{2,1,0:T(1,128)S(1)} async-done(((f32[8,1,6]{2,1,0:T(1,128)}), f32[8,1,6]{2,1,0:T(1,128)S(1)}, u32[]{:S(2)}, u32[]{:S(2)}) %all-to-all-start.3) | async-done | bytes 224 | tf_op jit(solution)/shard_map/all_to_all | solution.py:164
  197.9 3.3 %all-to-all-start.2 = ((f32[8,1,6]{2,1,0:T(1,128)}), f32[8,1,6]{2,1,0:T(1,128)S(1)}, u32[]{:S(2)}, u32[]{:S(2)}) async-start(f32[8,1,6]{2,1,0:T(1,128)} %bitcast.4), calls=%async_computation.2 | async-start | bytes 8192 | tf_op jit(solution)/shard_map/all_to_all | solution.py:157
  202.5 4.2 %all-to-all-done.2 = f32[8,1,6]{2,1,0:T(1,128)S(1)} async-done(((f32[8,1,6]{2,1,0:T(1,128)}), f32[8,1,6]{2,1,0:T(1,128)S(1)}, u32[]{:S(2)}, u32[]{:S(2)}) %all-to-all-start.2) | async-done | bytes 224 | tf_op jit(solution)/shard_map/all_to_all | solution.py:157
  209.0 3.3 %all-to-all-start.4 = ((f32[8,1,6]{2,1,0:T(1,128)}), f32[8,1,6]{2,1,0:T(1,128)S(1)}, u32[]{:S(2)}, u32[]{:S(2)}) async-start(f32[8,1,6]{2,1,0:T(1,128)} %bitcast.13), calls=%async_computation.4 | async-start | bytes 8192 | tf_op jit(solution)/shard_map/all_to_all | solution.py:183
  212.7 5.0 %all-to-all-done.4 = f32[8,1,6]{2,1,0:T(1,128)S(1)} async-done(((f32[8,1,6]{2,1,0:T(1,128)}), f32[8,1,6]{2,1,0:T(1,128)S(1)}, u32[]{:S(2)}, u32[]{:S(2)}) %all-to-all-start.4) | async-done | bytes 224 | tf_op jit(solution)/shard_map/all_to_all | solution.py:183
  218.6 28.0 %while.25 = (s32[]{:T(128)}, bf16[4,2,1,33024]{3,2,1,0:T(2,128)(2,1)}, s32[4]{0:T(128)S(1)}, bf16[48,5,8,1]{0,2,1,3:T(8,128)(2,1)S(1)}, bf16[48,33024]{1,0:T(8,1...) while((s32[]{:T(128)}, ...), condition=%wide.region_13.14_spmd.clone.clone, body=%wide.region_10.13_spmd.clone.clone.sunk | while | flops 34543108 | bytes 8065315 | solution.py:204
  220.4 3.1 %fusion.100 = (f32[5,16512]{1,0:T(8,128)S(1)}, f32[5,16512]{1,0:T(8,128)S(1)}) fusion(s32[5]{0:T(128)S(1)} %get-tuple-element.518, s32[16512]{0:T(1024)} %get-tuple-element.519, s32[5]{0:T(128)S(1)} %get-tuple-element.516, s32[16512]{0:T(1024)} %get-tuple-element.517), kind=kLoop, calls=%fused_computation.47.clone.1 | loop fusion | flops 1320960 | bytes 792616 | tf_op jit(solution)/shard_map/cos | solution.py:25
  223.5 0.9 add_reduce_fusion.3
  224.6 1.0 fusion.101
  227.4 3.1 %fusion.100 = (f32[5,16512]{1,0:T(8,128)S(1)}, f32[5,16512]{1,0:T(8,128)S(1)}) fusion(s32[5]{0:T(128)S(1)} %get-tuple-element.518, s32[16512]{0:T(1024)} %get-tuple-element.519, s32[5]{0:T(128)S(1)} %get-tuple-element.516, s32[16512]{0:T(1024)} %get-tuple-element.517), kind=kLoop, calls=%fused_computation.47.clone.1 | loop fusion | flops 1320960 | bytes 792616 | tf_op jit(solution)/shard_map/cos | solution.py:25
  230.5 0.9 add_reduce_fusion.3
  231.6 1.0 fusion.101
  234.4 3.1 %fusion.100 = (f32[5,16512]{1,0:T(8,128)S(1)}, f32[5,16512]{1,0:T(8,128)S(1)}) fusion(s32[5]{0:T(128)S(1)} %get-tuple-element.518, s32[16512]{0:T(1024)} %get-tuple-element.519, s32[5]{0:T(128)S(1)} %get-tuple-element.516, s32[16512]{0:T(1024)} %get-tuple-element.517), kind=kLoop, calls=%fused_computation.47.clone.1 | loop fusion | flops 1320960 | bytes 792616 | tf_op jit(solution)/shard_map/cos | solution.py:25
  237.5 0.9 add_reduce_fusion.3
  238.6 1.0 fusion.101
  241.4 3.1 %fusion.100 = (f32[5,16512]{1,0:T(8,128)S(1)}, f32[5,16512]{1,0:T(8,128)S(1)}) fusion(s32[5]{0:T(128)S(1)} %get-tuple-element.518, s32[16512]{0:T(1024)} %get-tuple-element.519, s32[5]{0:T(128)S(1)} %get-tuple-element.516, s32[16512]{0:T(1024)} %get-tuple-element.517), kind=kLoop, calls=%fused_computation.47.clone.1 | loop fusion | flops 1320960 | bytes 792616 | tf_op jit(solution)/shard_map/cos | solution.py:25
  244.5 0.9 add_reduce_fusion.3
  245.6 1.0 fusion.101
  246.6 4.8 %convert_reduce_fusion = bf16[4,2,33024]{2,1,0:T(2,128)(2,1)S(1)} fusion(bf16[4,2,1,33024]{3,2,1,0:T(2,128)(2,1)} %get-tuple-element.82), kind=kLoop, calls=%fused_computation.73 | loop fusion | bytes 1056768 | tf_op jit(solution)/shard_map/convert_element_type | solution.py:209
  251.4 1.0 convert_element_type.122
  253.7 42.7 %all-reduce.3.cloned.1.call-done = bf16[8,1,33024]{2,0,1:T(8,128)(2,1)} async-done(((bf16[8,1,33024]{2,0,1:T(8,128)(2,1)}), bf16[8,1,33024]{2,0,1:T(8,128)(2,1)}) %all-reduce.3.cloned.1.call-update) | async-done | bytes 528400
  296.4 1.8 constant_dynamic-slice_fusion.1
  (117 shorter events, 19.6 us)
Async XLA Ops:
  10.0 17.5 %all-to-all-start.1 = ((s32[8,1,6]{2,1,0:T(1,128)}), s32[8,1,6]{2,1,0:T(1,128)S(1)}, u32[]{:S(2)}, u32[]{:S(2)}) async-start(s32[8,1,6]{2,1,0:T(1,128)} %bitcast.3), calls=%async_computation.1 | async-start | bytes 8192 | tf_op jit(solution)/shard_map/all_to_all | solution.py:108
  27.5 5.2 %copy-start.3 = (bf16[2,1,33024]{2,0,1:T(2,128)(2,1)S(1)}, bf16[2,1,33024]{2,0,1:T(2,128)(2,1)}, u32[]{:S(2)}) copy-start(bf16[2,1,33024]{2,0,1:T(2,128)(2,1)} %param.13) | copy-start | bytes 396292
  27.5 100.0 %all-to-all-start = ((bf16[8,6,33024]{2,1,0:T(8,128)(2,1)}), bf16[8,6,33024]{2,1,0:T(8,128)(2,1)}, u32[]{:S(2)}, u32[]{:S(2)}) async-start(bf16[8,6,33024]{2,1,0:T(8,128)(2,1)} %reshape.281), calls=%async_computation | async-start | bytes 8454144 | tf_op jit(solution)/shard_map/all_to_all | solution.py:107
  48.2 4.2 %copy-start.2 = (bf16[8,16512]{1,0:T(8,128)(2,1)S(1)}, bf16[8,16512]{1,0:T(8,128)(2,1)}, u32[]{:S(2)}) copy-start(bf16[8,16512]{1,0:T(8,128)(2,1)} %param.14) | copy-start | bytes 792580
  53.4 77.0 %copy-start.4 = (s32[5]{0:T(128)S(1)}, s32[5]{0:T(128)}, u32[]{:S(2)}) copy-start(s32[5]{0:T(128)} %constant.95.clone) | copy-start | bytes 64
  53.4 77.0 %copy-start.5 = (s32[5]{0:T(128)S(1)}, s32[5]{0:T(128)}, u32[]{:S(2)}) copy-start(s32[5]{0:T(128)} %constant.96.clone) | copy-start | bytes 64
  134.5 0.7 copy-start
  140.1 2.2 copy-start.1
  149.0 0.7 copy-start
  154.6 2.2 copy-start.1
  163.5 0.7 copy-start
  169.1 2.2 copy-start.1
  177.9 0.7 copy-start
  183.6 2.2 copy-start.1
  189.1 8.9 %all-to-all-start.3 = ((f32[8,1,6]{2,1,0:T(1,128)}), f32[8,1,6]{2,1,0:T(1,128)S(1)}, u32[]{:S(2)}, u32[]{:S(2)}) async-start(f32[8,1,6]{2,1,0:T(1,128)} %bitcast.8), calls=%async_computation.3 | async-start | bytes 8192 | tf_op jit(solution)/shard_map/all_to_all | solution.py:164
  197.9 8.8 %all-to-all-start.2 = ((f32[8,1,6]{2,1,0:T(1,128)}), f32[8,1,6]{2,1,0:T(1,128)S(1)}, u32[]{:S(2)}, u32[]{:S(2)}) async-start(f32[8,1,6]{2,1,0:T(1,128)} %bitcast.4), calls=%async_computation.2 | async-start | bytes 8192 | tf_op jit(solution)/shard_map/all_to_all | solution.py:157
  208.2 10.4 %copy-start.6 = (f32[12]{0:T(128)}, f32[12]{0:T(128)S(1)}, u32[]{:S(2)}) copy-start(f32[12]{0:T(128)S(1)} %log_add_fusion) | copy-start | bytes 148
  209.0 8.8 %all-to-all-start.4 = ((f32[8,1,6]{2,1,0:T(1,128)}), f32[8,1,6]{2,1,0:T(1,128)S(1)}, u32[]{:S(2)}, u32[]{:S(2)}) async-start(f32[8,1,6]{2,1,0:T(1,128)} %bitcast.13), calls=%async_computation.4 | async-start | bytes 8192 | tf_op jit(solution)/shard_map/all_to_all | solution.py:183
  212.3 84.0 %all-reduce.3.cloned.1.call-start = ((), (), s32[]{:S(2)}) async-start(), calls=%async_computation.5 | async-start | bytes 1056768
  251.4 1.1 copy-start.7
Sparse Core Ops, SparseCore 0:
  252.5 43.7 all-reduce.2
where the time goes:
time: 307 us; the launch traced here: 305 us
  waiting for transfers between devices  131 us (43%)
  other arithmetic  46.6 us (15%)
  local copies, waits for them, and re-layouts  44 us (14%)
  matrix products  28.7 us (9%)
  starting transfers between devices  21.8 us (7%)
  blocking collectives  15.3 us (5%)
  between operations  14.9 us (5%)
    all_to_all x1, waiting for transfers between devices, per_device(): lax.all_to_all(send_images, 'orient', split_axis=0, concat_axis=0, tiled=...  74.1 us
    unnamed x2, waiting for transfers between devices  42.7 us
    cos x8, other arithmetic, rotation(): return (jnp.cos(angle), jnp.sin(angle))  24.6 us
    all_gather x1, blocking collectives, per_device(): ref_piece = lax.all_gather(projections, 'cls', axis=0, tiled=True)  15.3 us
    dot_general x4, matrix products, one_group(): lax.dot_general(ctf_square, magnitude.reshape(group_size * directions, pi...  9.16 us
    add x4, local copies, waits for them, and re-layouts, turn_refs(): second = real_ref[None] * sin_wide + imag_ref[None] * cos_wide  9.07 us
    dot_general x4, matrix products, one_group(): lax.dot_general(rows_in, turned.reshape(-1, 2 * pixel_count), (((1,), (1,...  8.57 us
    all_to_all x1, starting transfers between devices, per_device(): lax.all_to_all(send_codes, 'orient', split_axis=0, concat_axis=0, tiled=T...  6.35 us
  transfers between devices with their start and end apart: 6, of which 5 were waited for; matrix products, arithmetic and copies ran while one was open for 6% of the time, Pallas kernels for 0%

commit v1 on v0

--- a/solution.py
+++ b/solution.py
@@ -1,9 +1,11 @@
+import functools
 import math
 import jax
 import jax.numpy as jnp
 import numpy as np
 from jax import lax
 from jax.sharding import PartitionSpec as P
+from jax.lax import axis_index, axis_size, ppermute
 
 KX = 86
 KY = 192
@@ -12,6 +14,21 @@
 highest = lax.Precision.HIGHEST
 local_across = np.array([0, 1, -1, 0, 0], dtype=np.int32)
 local_down = np.array([0, 0, 0, 1, -1], dtype=np.int32)
+
+
+def open_the_area(sample, mesh_dim, dim_k):
+    world = axis_size(mesh_dim)
+    g_now = sorted(((dev_i, (dev_i + 1) % world) for dev_i in range(world)))
+    front = sample
+    pages = [front]
+    for rr in range(1, world):
+        front = ppermute(front, mesh_dim, g_now)
+        pages.insert(0, front)
+    seen_now = jnp.concatenate(pages, axis=dim_k)
+    return jnp.roll(seen_now, shift=(axis_index(mesh_dim) + 1) * sample.shape[dim_k], axis=dim_k)
+
+
+mix_face = functools.partial(open_the_area, mesh_dim="cls", dim_k=0)
 
 
 def frequencies():
@@ -121,7 +138,7 @@
     )
     shift_total = cos_shift.shape[0]
     ctf_square = ctf_table * ctf_table
-    ref_piece = lax.all_gather(projections, "cls", axis=0, tiled=True)
+    ref_piece = mix_face(projections)
     piece_rows = ref_piece.shape[0]
     group_size = 2
     grouped = ref_piece.reshape(piece_rows // group_size, group_size, directions, 2 * pixel_count)

time: 307 us -> 311 us (1.013)
  blocking collectives: 15.3 us -> 0 us
  waiting for transfers between devices: 131 us -> 145 us
  local copies, waits for them, and re-layouts: 44 us -> 49.4 us
  other arithmetic: 46.6 us -> 43.4 us
  starting transfers between devices: 21.8 us -> 25 us
    all_gather x1 -> x0, blocking collectives: 15.3 us -> none  [per_device(): ref_piece = lax.all_gather(projections, 'cls', axis=0, tiled=True)]
    all_to_all x1, waiting for transfers between devices: 74.1 us -> 87 us  [per_device(): lax.all_to_all(send_images, 'orient', split_axis=0, concat_axis=0, tiled=...]
    concatenate x0 -> x1, local copies, waits for them, and re-layouts: none -> 5.51 us  [open_the_area(): jnp.roll(seen_now, shift=(axis_index(mesh_dim) + 1) * sample.shape[dim_k]...]
    ppermute x0 -> x3, starting transfers between devices: none -> 5.15 us  [open_the_area(): front = ppermute(front, mesh_dim, g_now)]
    all_gather x1 -> x0, other arithmetic: 3.18 us -> none  [per_device(): ref_piece = lax.all_gather(projections, 'cls', axis=0, tiled=True)]
  transfers between devices with their start and end apart: 6 -> 9, of which waited for: 5 -> 6; matrix products, arithmetic and copies ran while one was open for 6% -> 7% of each run, Pallas kernels for 0% -> 0%
where the time goes in v1:
time: 311 us; the launch traced here: 310 us
  waiting for transfers between devices  145 us (47%)
  local copies, waits for them, and re-layouts  49.4 us (16%)
  other arithmetic  43.4 us (14%)
  matrix products  28.7 us (9%)
  starting transfers between devices  25 us (8%)
  between operations  14.9 us (5%)
    all_to_all x1, waiting for transfers between devices, per_device(): lax.all_to_all(send_images, 'orient', split_axis=0, concat_axis=0, tiled=...  87 us
    unnamed x2, waiting for transfers between devices  42.7 us
    cos x8, other arithmetic, rotation(): return (jnp.cos(angle), jnp.sin(angle))  24.6 us
    dot_general x4, matrix products, one_group(): lax.dot_general(ctf_square, magnitude.reshape(group_size * directions, pi...  9.16 us
    add x4, local copies, waits for them, and re-layouts, turn_refs(): second = real_ref[None] * sin_wide + imag_ref[None] * cos_wide  9.07 us
    dot_general x4, matrix products, one_group(): lax.dot_general(rows_in, turned.reshape(-1, 2 * pixel_count), (((1,), (1,...  8.57 us
  transfers between devices with their start and end apart: 9, of which 6 were waited for; matrix products, arithmetic and copies ran while one was open for 7% of the time, Pallas kernels for 0%

profile of v1, /device:TPU:0, one launch (start us, length us, event | category | flops | bytes accessed | tf_op | source)
XLA Modules:
  0.0 309.9 jit_solution(665000068920834455)
XLA Ops:
  7.2 3.0 collective-permute-start
  13.0 4.9 %all-to-all-start.1 = ((s32[8,1,6]{2,1,0:T(1,128)}), s32[8,1,6]{2,1,0:T(1,128)S(1)}, u32[]{:S(2)}, u32[]{:S(2)}) async-start(s32[8,1,6]{2,1,0:T(1,128)} %bitcast.3), calls=%async_computation.1 | async-start | bytes 8192 | tf_op jit(solution)/shard_map/all_to_all | solution.py:125
  19.3 6.1 %fusion.38 = (bf16[12,16512]{1,0:T(8,128)(2,1)S(1)}, bf16[12,16512]{1,0:T(8,128)(2,1)S(1)}) fusion(s32[12]{0:T(128)S(1)} %get-tuple-element.313, s32[16512]{0:T(1024)} %get-tuple-element.493, s32[12]{0:T(128)S(1)} %get-tuple-element.312, s32[16512]{0:T(1024)} %get-tuple-element.491, bf16[12,33024]{1,0:T(8,128)(2,1)} %param.12, bf16[8,16512]{1,0:T(8,128)(2,1)} %param.14, ...), kind=kOutput, calls=%fused_computation.63 | convolution fusion | flops 8718432 | bytes 1981584 | tf_op jit(solution)/shard_map/dot_general | solution.py:110
  25.5 1.5 collective-permute-start.1
  27.0 1.0 convolution_convert_fusion
  28.0 2.6 reshape.281
  30.6 1.7 collective-permute-done.1
  32.9 4.7 %all-to-all-start = ((bf16[8,6,33024]{2,1,0:T(8,128)(2,1)}), bf16[8,6,33024]{2,1,0:T(8,128)(2,1)}, u32[]{:S(2)}, u32[]{:S(2)}) async-start(bf16[8,6,33024]{2,1,0:T(8,128)(2,1)} %reshape.281), calls=%async_computation | async-start | bytes 8454144 | tf_op jit(solution)/shard_map/all_to_all | solution.py:124
  38.7 5.5 %concatenate.20 = bf16[16,1,33024]{2,0,1:T(8,128)(2,1)S(1)} concatenate(bf16[2,1,33024]{2,0,1:T(2,128)(2,1)S(1)} %collective-permute-done.2, bf16[2,1,33024]{2,0,1:T(2,128)(2,1)S(1)} %collective-permute-done.1, bf16[2,1,33024]{2,0,1:T(2,128)(2,1)S(1)} %collective-permute-done, bf16[2,1,33024]{2,0,1:T(2,128)(2,1)S(1)} %copy-done.2, ...), dimensions={0} | concatenate | bytes 2113536 | tf_op jit(solution)/shard_map/jit(_roll_dynamic)/concatenate | solution.py:28
  44.4 1.0 reshape.280
  45.4 87.0 %all-to-all-done = bf16[8,6,33024]{2,1,0:T(8,128)(2,1)} async-done(((bf16[8,6,33024]{2,1,0:T(8,128)(2,1)}), bf16[8,6,33024]{2,1,0:T(8,128)(2,1)}, u32[]{:S(2)}, u32[]{:S(2)}) %all-to-all-start) | async-done | bytes 3170336 | tf_op jit(solution)/shard_map/all_to_all | solution.py:124
  132.4 2.8 reshape.282
  135.3 57.9 %while.24 = (s32[]{:T(128)}, f32[4,48,5,2,1]{1,3,2,4,0:T(2,128)S(1)}, bf16[4,2,1,33024]{3,1,2,0:T(2,128)(2,1)}, bf16[48,33024]{1,0:T(8,128)(2,1)S(1)}, f32[8,165...) while((s32[]{:T(128)}, ...), condition=%wide.region_5.6_spmd.clone.clone, body=%wide.region_4.5_spmd.clone.clone.sunk | while | flops 39077952 | bytes 9925141 | solution.py:167
  135.3 3.1 fusion.95
  138.4 1.0 dynamic-slice_bitcast_fusion.2
  140.0 1.4 subtract_convert_fusion.2
  141.5 2.3 add.667
  143.7 1.3 sub.147
  145.0 2.1 convolution_bitcast_fusion.5
  147.2 2.3 fusion.96
  149.8 3.1 fusion.95
  152.9 1.0 dynamic-slice_bitcast_fusion.2
  154.5 1.4 subtract_convert_fusion.2
  155.9 2.3 add.667
  158.2 1.3 sub.147
  159.5 2.1 convolution_bitcast_fusion.5
  161.7 2.3 fusion.96
  164.3 3.1 fusion.95
  167.3 1.0 dynamic-slice_bitcast_fusion.2
  169.0 1.4 subtract_convert_fusion.2
  170.4 2.3 add.667
  172.7 1.3 sub.147
  174.0 2.1 convolution_bitcast_fusion.5
  176.2 2.3 fusion.96
  178.7 3.1 fusion.95
  181.8 1.0 dynamic-slice_bitcast_fusion.2
  183.5 1.4 subtract_convert_fusion.2
  184.9 2.3 add.667
  187.2 1.3 sub.147
  188.5 2.1 convolution_bitcast_fusion.5
  190.7 2.3 fusion.96
  194.0 3.3 %all-to-all-start.3 = ((f32[8,1,6]{2,1,0:T(1,128)}), f32[8,1,6]{2,1,0:T(1,128)S(1)}, u32[]{:S(2)}, u32[]{:S(2)}) async-start(f32[8,1,6]{2,1,0:T(1,128)} %bitcast.8), calls=%async_computation.3 | async-start | bytes 8192 | tf_op jit(solution)/shard_map/all_to_all | solution.py:181
  198.1 4.7 %all-to-all-done.3 = f32[8,1,6]{2,1,0:T(1,128)S(1)} async-done(((f32[8,1,6]{2,1,0:T(1,128)}), f32[8,1,6]{2,1,0:T(1,128)S(1)}, u32[]{:S(2)}, u32[]{:S(2)}) %all-to-all-start.3) | async-done | bytes 224 | tf_op jit(solution)/shard_map/all_to_all | solution.py:181
  202.8 3.3 %all-to-all-start.2 = ((f32[8,1,6]{2,1,0:T(1,128)}), f32[8,1,6]{2,1,0:T(1,128)S(1)}, u32[]{:S(2)}, u32[]{:S(2)}) async-start(f32[8,1,6]{2,1,0:T(1,128)} %bitcast.4), calls=%async_computation.2 | async-start | bytes 8192 | tf_op jit(solution)/shard_map/all_to_all | solution.py:174
  207.4 4.2 %all-to-all-done.2 = f32[8,1,6]{2,1,0:T(1,128)S(1)} async-done(((f32[8,1,6]{2,1,0:T(1,128)}), f32[8,1,6]{2,1,0:T(1,128)S(1)}, u32[]{:S(2)}, u32[]{:S(2)}) %all-to-all-start.2) | async-done | bytes 224 | tf_op jit(solution)/shard_map/all_to_all | solution.py:174
  213.9 3.3 %all-to-all-start.4 = ((f32[8,1,6]{2,1,0:T(1,128)}), f32[8,1,6]{2,1,0:T(1,128)S(1)}, u32[]{:S(2)}, u32[]{:S(2)}) async-start(f32[8,1,6]{2,1,0:T(1,128)} %bitcast.13), calls=%async_computation.4 | async-start | bytes 8192 | tf_op jit(solution)/shard_map/all_to_all | solution.py:200
  217.6 5.0 %all-to-all-done.4 = f32[8,1,6]{2,1,0:T(1,128)S(1)} async-done(((f32[8,1,6]{2,1,0:T(1,128)}), f32[8,1,6]{2,1,0:T(1,128)S(1)}, u32[]{:S(2)}, u32[]{:S(2)}) %all-to-all-start.4) | async-done | bytes 224 | tf_op jit(solution)/shard_map/all_to_all | solution.py:200
  223.5 28.0 %while.25 = (s32[]{:T(128)}, bf16[4,2,1,33024]{3,2,1,0:T(2,128)(2,1)}, s32[4]{0:T(128)S(1)}, bf16[48,5,8,1]{0,2,1,3:T(8,128)(2,1)S(1)}, bf16[48,33024]{1,0:T(8,1...) while((s32[]{:T(128)}, ...), condition=%wide.region_13.14_spmd.clone.clone, body=%wide.region_10.13_spmd.clone.clone.sunk | while | flops 34543108 | bytes 8065315 | solution.py:221
  225.3 3.1 fusion.100
  228.4 0.9 add_reduce_fusion.3
  229.5 1.0 fusion.101
  232.3 3.1 fusion.100
  235.4 0.9 add_reduce_fusion.3
  236.5 1.0 fusion.101
  239.3 3.1 fusion.100
  242.4 0.9 add_reduce_fusion.3
  243.5 1.0 fusion.101
  246.3 3.1 fusion.100
  249.4 0.9 add_reduce_fusion.3
  250.5 1.0 fusion.101
  251.5 4.8 %convert_reduce_fusion = bf16[4,2,33024]{2,1,0:T(2,128)(2,1)S(1)} fusion(bf16[4,2,1,33024]{3,2,1,0:T(2,128)(2,1)} %get-tuple-element.82), kind=kLoop, calls=%fused_computation.73 | loop fusion | bytes 1056768 | tf_op jit(solution)/shard_map/convert_element_type | solution.py:226
  256.3 1.0 convert_element_type.122
  258.6 42.6 %all-reduce.3.cloned.1.call-done = bf16[8,1,33024]{2,0,1:T(8,128)(2,1)} async-done(((bf16[8,1,33024]{2,0,1:T(8,128)(2,1)}), bf16[8,1,33024]{2,0,1:T(8,128)(2,1)}) %all-reduce.3.cloned.1.call-update) | async-done | bytes 528400
  301.2 1.8 constant_dynamic-slice_fusion.1
  (122 shorter events, 21.8 us)
Async XLA Ops:
  7.2 18.3 %collective-permute-start = (bf16[2,1,33024]{2,0,1:T(2,128)(2,1)}, bf16[2,1,33024]{2,0,1:T(2,128)(2,1)S(1)}, u32[]{:S(2)}, u32[]{:S(2)}) collective-permute-start(bf16[2,1,33024]{2,0,1:T(2,128)(2,1)} %param.13), channel_id=1, source_target_pairs={{0,1},{1,2},{2,3},{3,0},{4,5},{5,6},{6,7},{7,4},{8,9},{9,10},{10,1... | collective-permute-start | bytes 396296 | tf_op jit(solution)/shard_map/ppermute | solution.py:25
  13.0 19.9 %all-to-all-start.1 = ((s32[8,1,6]{2,1,0:T(1,128)}), s32[8,1,6]{2,1,0:T(1,128)S(1)}, u32[]{:S(2)}, u32[]{:S(2)}) async-start(s32[8,1,6]{2,1,0:T(1,128)} %bitcast.3), calls=%async_computation.1 | async-start | bytes 8192 | tf_op jit(solution)/shard_map/all_to_all | solution.py:125
  25.5 6.9 %collective-permute-start.1 = (bf16[2,1,33024]{2,0,1:T(2,128)(2,1)S(1)}, bf16[2,1,33024]{2,0,1:T(2,128)(2,1)S(1)}, u32[]{:S(2)}, u32[]{:S(2)}) collective-permute-start(bf16[2,1,33024]{2,0,1:T(2,128)(2,1)S(1)} %collective-permute-done), channel_id=1, source_target_pairs={{0,1},{1,2},{2,3},{3,0},{4,5},{5,6},{6,7},{7,4},{8,9},{9,10},{10,1... | collective-permute-start | bytes 396296 | tf_op jit(solution)/shard_map/ppermute | solution.py:25
  30.6 7.1 %copy-start.3 = (bf16[8,16512]{1,0:T(8,128)(2,1)S(1)}, bf16[8,16512]{1,0:T(8,128)(2,1)}, u32[]{:S(2)}) copy-start(bf16[8,16512]{1,0:T(8,128)(2,1)} %param.14) | copy-start | bytes 792580
  30.6 8.1 %copy-start.2 = (bf16[2,1,33024]{2,0,1:T(2,128)(2,1)S(1)}, bf16[2,1,33024]{2,0,1:T(2,128)(2,1)}, u32[]{:S(2)}) copy-start(bf16[2,1,33024]{2,0,1:T(2,128)(2,1)} %param.13) | copy-start | bytes 396292
  32.3 6.3 %collective-permute-start.2 = (bf16[2,1,33024]{2,0,1:T(2,128)(2,1)S(1)}, bf16[2,1,33024]{2,0,1:T(2,128)(2,1)S(1)}, u32[]{:S(2)}, u32[]{:S(2)}) collective-permute-start(bf16[2,1,33024]{2,0,1:T(2,128)(2,1)S(1)} %collective-permute-done.1), channel_id=1, source_target_pairs={{0,1},{1,2},{2,3},{3,0},{4,5},{5,6},{6,7},{7,4},{8,9},{9,10},{10,1... | collective-permute-start | bytes 396296 | tf_op jit(solution)/shard_map/ppermute | solution.py:25
  32.9 99.5 %all-to-all-start = ((bf16[8,6,33024]{2,1,0:T(8,128)(2,1)}), bf16[8,6,33024]{2,1,0:T(8,128)(2,1)}, u32[]{:S(2)}, u32[]{:S(2)}) async-start(bf16[8,6,33024]{2,1,0:T(8,128)(2,1)} %reshape.281), calls=%async_computation | async-start | bytes 8454144 | tf_op jit(solution)/shard_map/all_to_all | solution.py:124
  45.4 89.9 %copy-start.4 = (s32[5]{0:T(128)S(1)}, s32[5]{0:T(128)}, u32[]{:S(2)}) copy-start(s32[5]{0:T(128)} %constant.123.clone) | copy-start | bytes 64
  45.4 89.9 %copy-start.5 = (s32[5]{0:T(128)S(1)}, s32[5]{0:T(128)}, u32[]{:S(2)}) copy-start(s32[5]{0:T(128)} %constant.124.clone) | copy-start | bytes 64
  139.4 0.7 copy-start
  145.0 2.2 copy-start.1
  153.9 0.7 copy-start
  159.5 2.2 copy-start.1
  168.4 0.7 copy-start
  174.0 2.2 copy-start.1
  182.8 0.7 copy-start
  188.5 2.2 copy-start.1
  194.0 8.9 %all-to-all-start.3 = ((f32[8,1,6]{2,1,0:T(1,128)}), f32[8,1,6]{2,1,0:T(1,128)S(1)}, u32[]{:S(2)}, u32[]{:S(2)}) async-start(f32[8,1,6]{2,1,0:T(1,128)} %bitcast.8), calls=%async_computation.3 | async-start | bytes 8192 | tf_op jit(solution)/shard_map/all_to_all | solution.py:181
  202.8 8.8 %all-to-all-start.2 = ((f32[8,1,6]{2,1,0:T(1,128)}), f32[8,1,6]{2,1,0:T(1,128)S(1)}, u32[]{:S(2)}, u32[]{:S(2)}) async-start(f32[8,1,6]{2,1,0:T(1,128)} %bitcast.4), calls=%async_computation.2 | async-start | bytes 8192 | tf_op jit(solution)/shard_map/all_to_all | solution.py:174
  213.1 10.4 %copy-start.6 = (f32[12]{0:T(128)}, f32[12]{0:T(128)S(1)}, u32[]{:S(2)}) copy-start(f32[12]{0:T(128)S(1)} %log_add_fusion) | copy-start | bytes 148
  213.9 8.8 %all-to-all-start.4 = ((f32[8,1,6]{2,1,0:T(1,128)}), f32[8,1,6]{2,1,0:T(1,128)S(1)}, u32[]{:S(2)}, u32[]{:S(2)}) async-start(f32[8,1,6]{2,1,0:T(1,128)} %bitcast.13), calls=%async_computation.4 | async-start | bytes 8192 | tf_op jit(solution)/shard_map/all_to_all | solution.py:200
  217.2 83.9 %all-reduce.3.cloned.1.call-start = ((), (), s32[]{:S(2)}) async-start(), calls=%async_computation.5 | async-start | bytes 1056768
  256.3 1.1 copy-start.7
Sparse Core Ops, SparseCore 0:
  257.4 43.7 all-reduce.2
